TPU v7x, 32 devices: a whole 2x2x4 slice. The times are simulated.
32 devices in a mesh: wide: 8 (over z, core), narrow: 4 (over y, x).
Axes of the slice: x: 2, y: 2, z: 4, core: 2. Of those that a mesh axis runs over, the one named last changes fastest.
Arguments:
- homolog_embedding: float32 [32, 1024, 256], P('wide', 'narrow'), may hold values from -6 to 6
- pair_state: float32 [1024, 1024, 128], P('wide', 'narrow'), may hold values from -6 to 6
- probe_projector: float32 [256, 256], replicated, may hold values from -0.375 to 0.375
- lookup_projector: float32 [256, 256], replicated, may hold values from -0.375 to 0.375
- content_projector: float32 [256, 256], replicated, may hold values from -0.375 to 0.375
- sigmoid_projector: float32 [256, 256], replicated, may hold values from -0.375 to 0.375
- sigmoid_offset: float32 [256], replicated, may hold values from -4 to 4
- pair_bias_weight: float32 [128, 8], replicated, may hold values from -4 to 4
- mixing_projector: float32 [256, 256], replicated, may hold values from -0.375 to 0.375
- mixing_offset: float32 [256], replicated, may hold values from -3 to 3
- first_factor_projector: float32 [256, 32], replicated, may hold values from -0.375 to 0.375
- second_factor_projector: float32 [256, 32], replicated, may hold values from -0.375 to 0.375
- outer_product_weight: float32 [1024, 128], replicated, may hold values from -0.5 to 0.5
- outer_product_bias: float32 [128], replicated, may hold values from -3 to 3
- up_weight: float32 [128, 512], replicated, may hold values from -0.5 to 0.5
- expand_bias: float32 [512], replicated, may hold values from -3 to 3
- down_weight: float32 [512, 128], replicated, may hold values from -0.25 to 0.25
Outputs:
- alignment_state_next: float32 [32, 1024, 256], P('wide', 'narrow')
- pair_state_next: float32 [1024, 1024, 128], P('wide', 'narrow')
All inputs are finite; a program needn't handle non-finite values.
Results may differ from a plain program's by a relative error of at most 0.0003.
Values sent between devices are 32-bit elements; how exact they have to be, the bound alone decides.
No kernel may reach another device: no remote copies, remote signals or barrier semaphores. Data moves between devices by JAX's collectives and lax.ppermute only.
A program may use at most 192 MiB of HBM per device.

v0:
```python
import math
import jax
import jax.numpy as jnp
from jax import lax
from jax.sharding import PartitionSpec as P

finest_precision = lax.Precision.HIGHEST


def layer_normalize(tensor):
    row_mean = jnp.mean(tensor, axis=-1, keepdims=True)
    centered = tensor - row_mean
    variance = jnp.mean(centered * centered, axis=-1, keepdims=True)
    return centered * lax.rsqrt(variance + 1e-05)


def matrix_multiply(first_arr, second_arr):
    return jnp.dot(
        first_arr, second_arr, precision=finest_precision, preferred_element_type=jnp.float32
    )


def per_device(
    homolog_embedding,
    pair_state,
    probe_projector,
    lookup_projector,
    content_projector,
    sigmoid_projector,
    sigmoid_offset,
    pair_bias_weight,
    mixing_projector,
    mixing_offset,
    first_factor_projector,
    second_factor_projector,
    outer_product_weight,
    outer_product_bias,
    up_weight,
    expand_bias,
    down_weight,
):
    head_count = pair_bias_weight.shape[1]
    channel_count = homolog_embedding.shape[2]
    head_width = channel_count // head_count
    alignment_normed = layer_normalize(homolog_embedding)
    query_vectors = matrix_multiply(alignment_normed, probe_projector) / math.sqrt(head_width)
    key_rows = matrix_multiply(alignment_normed, lookup_projector)
    value_rows = matrix_multiply(alignment_normed, content_projector)
    gate_logits = matrix_multiply(alignment_normed, sigmoid_projector) + sigmoid_offset
    bias_tile = jnp.einsum(
        "ijc,ch->hij", layer_normalize(pair_state), pair_bias_weight, precision=finest_precision
    )
    own_heads = lax.all_to_all(bias_tile, "narrow", split_axis=0, concat_axis=2, tiled=True)
    pair_bias = lax.all_gather(own_heads, "wide", axis=1, tiled=True)
    operands = (
        lax.all_to_all(query_vectors, "narrow", split_axis=2, concat_axis=1, tiled=True),
        lax.all_to_all(key_rows, "narrow", split_axis=2, concat_axis=1, tiled=True),
        lax.all_to_all(value_rows, "narrow", split_axis=2, concat_axis=1, tiled=True),
        lax.all_to_all(gate_logits, "narrow", split_axis=2, concat_axis=1, tiled=True),
    )
    seq_len = operands[0].shape[1]
    local_width = operands[0].shape[2]
    local_heads = pair_bias.shape[0]
    local_size = local_width // local_heads
    row_span = min(512, seq_len)
    span_count = seq_len // row_span

    def per_item(item_parts):
        query_item = item_parts[0].reshape(seq_len, local_heads, local_size)
        key_item = item_parts[1].reshape(seq_len, local_heads, local_size)
        value_item = item_parts[2].reshape(seq_len, local_heads, local_size)

        def per_block(block_index):
            query_rows = lax.dynamic_slice_in_dim(query_item, block_index * row_span, row_span, 0)
            bias_rows = lax.dynamic_slice_in_dim(pair_bias, block_index * row_span, row_span, 1)
            scores = (
                jnp.einsum("qhd,khd->hqk", query_rows, key_item, precision=finest_precision)
                + bias_rows
            )
            row_max = jnp.max(scores, axis=-1, keepdims=True)
            exponent = jnp.exp(scores - row_max)
            softmax_probabilities = exponent / jnp.sum(exponent, axis=-1, keepdims=True)
            returned_tensor = jnp.einsum(
                "hqk,khd->qhd", softmax_probabilities, value_item, precision=finest_precision
            )
            return returned_tensor.reshape(row_span, local_width)

        blocks = lax.map(per_block, jnp.arange(span_count, dtype=jnp.int32))
        return blocks.reshape(seq_len, local_width)

    outcome = lax.map(per_item, (operands[0], operands[1], operands[2]))
    outcome = outcome * jax.nn.sigmoid(operands[3])
    merged_heads = lax.all_to_all(outcome, "narrow", split_axis=1, concat_axis=2, tiled=True)
    alignment_state_next = (
        homolog_embedding + matrix_multiply(merged_heads, mixing_projector) + mixing_offset
    )
    outer_product_normed = layer_normalize(alignment_state_next)
    left_proj = jnp.einsum(
        "srm,mc->scr", outer_product_normed, first_factor_projector, precision=finest_precision
    )
    right_proj = jnp.einsum(
        "srm,mc->scr", outer_product_normed, second_factor_projector, precision=finest_precision
    )
    left_rows = lax.all_gather(left_proj, "narrow", axis=2, tiled=True)
    left_all = lax.all_to_all(left_rows, "wide", split_axis=2, concat_axis=0, tiled=True)
    seq_count = left_all.shape[0]
    tile_rows = left_all.shape[2]
    tile_cols = right_proj.shape[2]
    outer_width = left_all.shape[1] * right_proj.shape[1]
    right_all = lax.all_gather(right_proj, "wide", axis=0, tiled=True)
    block_rows = math.gcd(16, tile_rows)

    def outer_block(block_index):
        left_part = lax.dynamic_slice_in_dim(left_all, block_index * block_rows, block_rows, 2)
        product = (
            jnp.einsum("sci,sdj->ijcd", left_part, right_all, precision=finest_precision)
            / seq_count
        )
        flat = product.reshape(block_rows * tile_cols, outer_width)
        return matrix_multiply(flat, outer_product_weight).reshape(block_rows, tile_cols, -1)

    update = lax.map(outer_block, jnp.arange(tile_rows // block_rows, dtype=jnp.int32))
    update = update.reshape(tile_rows, tile_cols, -1)
    pair_mid = pair_state + update + outer_product_bias
    hidden = jax.nn.relu(matrix_multiply(layer_normalize(pair_mid), up_weight) + expand_bias)
    pair_state_next = pair_mid + matrix_multiply(hidden, down_weight)
    return (alignment_state_next, pair_state_next)


def solution(mesh):
    placed = (
        P("wide", "narrow", None),
        P("wide", "narrow", None),
        P(),
        P(),
        P(),
        P(),
        P(),
        P(),
        P(),
        P(),
        P(),
        P(),
        P(),
        P(),
        P(),
        P(),
        P(),
    )
    return jax.shard_map(
        per_device,
        mesh=mesh,
        in_specs=placed,
        out_specs=(P("wide", "narrow", None), P("wide", "narrow", None)),
        check_vma=False,
    )
```

profile of v0, /device:TPU:0, one launch (start us, length us, event | category | flops | bytes accessed | tf_op | source)
XLA Modules:
  0.0 893.6 jit_solution(2013924085573206081)
XLA Ops:
  7.2 8.2 reduce_sum.83
  15.5 11.2 %multiply_reduce_fusion.1 = f32[128,256]{1,0:T(8,128)S(1)} fusion(f32[128,256,128]{2,1,0:T(8,128)} %param.24, f32[128,256]{1,0:T(8,128)S(1)} %broadcast_multiply_fusion.1), kind=kLoop, calls=%fused_computation.34 | loop fusion | flops 12550144 | bytes 17039360 | tf_op jit(solution)/shard_map/reduce_sum | solution.py:13
  26.8 27.4 %fusion.36 = f32[8,128,256]{2,0,1:T(8,128)S(1)} fusion(f32[128,256,128]{2,1,0:T(8,128)S(1)} %copy-done.1, f32[128,256]{1,0:T(8,128)S(1)} %add_rsqrt_fusion.1, f32[128,256]{1,0:T(8,128)S(1)} %broadcast_multiply_fusion.1, f32[128,8]{0,1:T(8,128)S(1)} %copy-done.11), kind=kOutput, calls=%fused_computation.49 | convolution fusion | flops 411041792 | bytes 18092032 | tf_op jit(solution)/shard_map/ijc,ch->hij/dot_general | solution.py:50
  54.6 19.1 %all_to_all.117 = f32[8,128,256]{2,1,0:T(8,128)S(1)} all-to-all(f32[8,128,256]{2,1,0:T(8,128)S(1)} %copy.112), channel_id=1, replica_groups=mesh['wide'=8,'narrow'=4] {'narrow'}, dimensions={0} | all-to-all | bytes 2097152 | tf_op jit(solution)/shard_map/all_to_all | solution.py:53
  77.8 3.5 all-to-all-start.4
  84.7 9.1 %all-to-all-done.4 = f32[4,256,256]{1,0,2:T(4,128)S(1)} async-done(((f32[4,256,256]{1,0,2:T(4,128)}), f32[4,256,256]{1,0,2:T(4,128)S(1)}, u32[]{:S(2)}, u32[]{:S(2)}) %all-to-all-start.4) | async-done | bytes 1048608 | tf_op jit(solution)/shard_map/all_to_all | solution.py:59
  93.8 3.5 all-to-all-start.2
  102.9 7.6 all-to-all-done.2
  110.5 4.3 all-to-all-start.1
  114.8 3.0 convolution_multiply_fusion.1
  120.3 7.8 all-to-all-done.1
  128.1 4.0 all-to-all-start
  137.5 7.7 all-to-all-done
  145.6 11.1 %all-gather.3.cloned.1.call-done = f32[2,1024,1024]{2,1,0:T(8,128)} async-done(((f32[2,128,1024]{2,1,0:T(8,128)}), f32[2,1024,1024]{2,1,0:T(8,128)}) %all-gather.3.cloned.1.call-update) | async-done | bytes 8388624 | tf_op jit(solution)/shard_map/all_gather | solution.py:54
  156.8 111.2 %while.31 = (s32[]{:T(128)}, f32[4,1024,64]{1,2,0:T(8,128)}, f32[4,1024,64]{1,2,0:T(8,128)S(1)}, f32[4,1024,64]{1,2,0:T(8,128)}, f32[4,1024,64]{1,2,0:T(8,128)},...) while((s32[]{:T(128)}, f32[4,1024,64]{1,2,0:T(8,128)}, ...), condition=%wide.region_9.10_spmd, body=%wide.region_4.9_spmd.sunk | while | flops 811595776 | bytes 20993444 | solution.py:91
  157.9 25.5 %while.33 = (s32[]{:T(128)}, f32[2,512,64]{1,2,0:T(8,128)S(1)}, s32[2]{0:T(128)S(1)}, f32[1024,2,32]{0,2,1:T(8,128)S(1)}, f32[1024,2,32]{0,2,1:T(8,128)S(1)}, /*...) while((s32[]{:T(128)}, f32[2,512,64]{1,2,0:T(8,128)S(1)}, ...), condition=%wide.region_8.8_spmd, body=%wide.region_5.7_spmd.sunk | while | flops 811595776 | bytes 17847476 | solution.py:88
  159.2 5.7 fusion.99
  166.1 4.6 fusion.101
  172.0 5.7 fusion.99
  178.9 4.6 fusion.101
  185.7 25.5 %while.33 = (s32[]{:T(128)}, f32[2,512,64]{1,2,0:T(8,128)S(1)}, s32[2]{0:T(128)S(1)}, f32[1024,2,32]{0,2,1:T(8,128)S(1)}, f32[1024,2,32]{0,2,1:T(8,128)S(1)}, /*...) while((s32[]{:T(128)}, f32[2,512,64]{1,2,0:T(8,128)S(1)}, ...), condition=%wide.region_8.8_spmd, body=%wide.region_5.7_spmd.sunk | while | flops 811595776 | bytes 17847476 | solution.py:88
  187.0 5.7 fusion.99
  193.9 4.6 fusion.101
  199.8 5.7 fusion.99
  206.7 4.6 fusion.101
  213.5 25.5 %while.33 = (s32[]{:T(128)}, f32[2,512,64]{1,2,0:T(8,128)S(1)}, s32[2]{0:T(128)S(1)}, f32[1024,2,32]{0,2,1:T(8,128)S(1)}, f32[1024,2,32]{0,2,1:T(8,128)S(1)}, /*...) while((s32[]{:T(128)}, f32[2,512,64]{1,2,0:T(8,128)S(1)}, ...), condition=%wide.region_8.8_spmd, body=%wide.region_5.7_spmd.sunk | while | flops 811595776 | bytes 17847476 | solution.py:88
  214.8 5.7 fusion.99
  221.7 4.6 fusion.101
  227.6 5.7 fusion.99
  234.4 4.6 fusion.101
  241.3 25.5 %while.33 = (s32[]{:T(128)}, f32[2,512,64]{1,2,0:T(8,128)S(1)}, s32[2]{0:T(128)S(1)}, f32[1024,2,32]{0,2,1:T(8,128)S(1)}, f32[1024,2,32]{0,2,1:T(8,128)S(1)}, /*...) while((s32[]{:T(128)}, f32[2,512,64]{1,2,0:T(8,128)S(1)}, ...), condition=%wide.region_8.8_spmd, body=%wide.region_5.7_spmd.sunk | while | flops 811595776 | bytes 17847476 | solution.py:88
  242.6 5.7 fusion.99
  249.5 4.6 fusion.101
  255.4 5.7 fusion.99
  262.2 4.6 fusion.101
  275.5 3.6 all-to-all-start.5
  280.6 12.7 %all-to-all-done.5 = f32[4,1,65536]{2,1,0:T(1,128)S(1)} async-done(((f32[4,1,65536]{2,1,0:T(1,128)}), f32[4,1,65536]{2,1,0:T(1,128)S(1)}, u32[]{:S(2)}, u32[]{:S(2)}) %all-to-all-start.5) | async-done | bytes 1048608 | tf_op jit(solution)/shard_map/all_to_all | solution.py:93
  293.8 4.6 reduce
  308.0 10.5 %all_gather.10 = f32[4,32,1024]{2,1,0:T(8,128)S(1)} all-gather(f32[4,32,256]{2,1,0:T(8,128)S(1)} %convolution_bitcast_fusion.1), channel_id=1, replica_groups=mesh['wide'=8,'narrow'=4] {'narrow'}, dimensions={2}, use_global_device_ids=true | all-gather | bytes 655360 | tf_op jit(solution)/shard_map/all_gather | solution.py:104
  320.2 3.5 reshape.119
  323.7 3.9 all-to-all-start.6
  328.9 13.9 %all-to-all-done.6 = f32[8,1,16384]{2,1,0:T(1,128)S(1)} async-done(((f32[8,1,16384]{2,1,0:T(1,128)}), f32[8,1,16384]{2,1,0:T(1,128)S(1)}, u32[]{:S(2)}, u32[]{:S(2)}) %all-to-all-start.6) | async-done | bytes 524320 | tf_op jit(solution)/shard_map/all_to_all | solution.py:105
  350.4 393.9 %while.32 = (s32[]{:T(128)}, f32[8,16,256,128]{3,2,1,0:T(8,128)}, s32[8]{0:T(128)S(1)}, f32[32,32,128]{0,2,1:T(8,128)}, f32[32,32,256]{2,0,1:T(8,128)S(1)}, /*in...) while((s32[]{:T(128)}, f32[8,16,256,128]{3,2,1,0:T(8,128)}, ...), condition=%wide.region_13.14_spmd, body=%wide.region_12.13_spmd.sunk | while | flops 8057257984 | bytes 37486768 | solution.py:122
  351.7 14.4 %convolution_multiply_fusion.3 = f32[32,16,32,256]{3,1,2,0:T(8,128)S(1)} fusion(f32[32,32,256]{2,0,1:T(8,128)S(1)} %get-tuple-element.424, f32[32,32,128]{0,2,1:T(8,128)} %get-tuple-element.423, s32[]{:T(128)S(6)} %select_n.9), kind=kOutput, calls=%fused_computation.16.clone.1 | convolution fusion | flops 1614807040 | bytes 18087940 | tf_op jit(solution)/shard_map/while/body/eval_jaxpr/sci,sdj->ijcd/dot_general | solution.py:116
  366.1 32.8 %bitcast_dynamic-update-slice_fusion.4 = f32[8,16,256,128]{3,2,1,0:T(8,128)} fusion(f32[8,16,256,128]{3,2,1,0:T(8,128)} %get-tuple-element.411, s32[]{:T(128)S(6)} %copy.191, f32[16,256,1024]{1,0,2:T(8,128)S(1)} %bitcast.139, f32[1024,128]{1,0:T(8,128)S(1)} %get-tuple-element.425), kind=kOutput, calls=%fused_computation.17.clone.1 | convolution fusion | flops 6442450944 | bytes 19398660 | tf_op jit(solution)/shard_map/while/body/eval_jaxpr/dot_general | solution.py:18
  400.1 14.4 %convolution_multiply_fusion.3 = f32[32,16,32,256]{3,1,2,0:T(8,128)S(1)} fusion(f32[32,32,256]{2,0,1:T(8,128)S(1)} %get-tuple-element.424, f32[32,32,128]{0,2,1:T(8,128)} %get-tuple-element.423, s32[]{:T(128)S(6)} %select_n.9), kind=kOutput, calls=%fused_computation.16.clone.1 | convolution fusion | flops 1614807040 | bytes 18087940 | tf_op jit(solution)/shard_map/while/body/eval_jaxpr/sci,sdj->ijcd/dot_general | solution.py:116
  414.5 32.8 %bitcast_dynamic-update-slice_fusion.4 = f32[8,16,256,128]{3,2,1,0:T(8,128)} fusion(f32[8,16,256,128]{3,2,1,0:T(8,128)} %get-tuple-element.411, s32[]{:T(128)S(6)} %copy.191, f32[16,256,1024]{1,0,2:T(8,128)S(1)} %bitcast.139, f32[1024,128]{1,0:T(8,128)S(1)} %get-tuple-element.425), kind=kOutput, calls=%fused_computation.17.clone.1 | convolution fusion | flops 6442450944 | bytes 19398660 | tf_op jit(solution)/shard_map/while/body/eval_jaxpr/dot_general | solution.py:18
  448.4 14.4 %convolution_multiply_fusion.3 = f32[32,16,32,256]{3,1,2,0:T(8,128)S(1)} fusion(f32[32,32,256]{2,0,1:T(8,128)S(1)} %get-tuple-element.424, f32[32,32,128]{0,2,1:T(8,128)} %get-tuple-element.423, s32[]{:T(128)S(6)} %select_n.9), kind=kOutput, calls=%fused_computation.16.clone.1 | convolution fusion | flops 1614807040 | bytes 18087940 | tf_op jit(solution)/shard_map/while/body/eval_jaxpr/sci,sdj->ijcd/dot_general | solution.py:116
  462.8 32.8 %bitcast_dynamic-update-slice_fusion.4 = f32[8,16,256,128]{3,2,1,0:T(8,128)} fusion(f32[8,16,256,128]{3,2,1,0:T(8,128)} %get-tuple-element.411, s32[]{:T(128)S(6)} %copy.191, f32[16,256,1024]{1,0,2:T(8,128)S(1)} %bitcast.139, f32[1024,128]{1,0:T(8,128)S(1)} %get-tuple-element.425), kind=kOutput, calls=%fused_computation.17.clone.1 | convolution fusion | flops 6442450944 | bytes 19398660 | tf_op jit(solution)/shard_map/while/body/eval_jaxpr/dot_general | solution.py:18
  496.8 14.4 %convolution_multiply_fusion.3 = f32[32,16,32,256]{3,1,2,0:T(8,128)S(1)} fusion(f32[32,32,256]{2,0,1:T(8,128)S(1)} %get-tuple-element.424, f32[32,32,128]{0,2,1:T(8,128)} %get-tuple-element.423, s32[]{:T(128)S(6)} %select_n.9), kind=kOutput, calls=%fused_computation.16.clone.1 | convolution fusion | flops 1614807040 | bytes 18087940 | tf_op jit(solution)/shard_map/while/body/eval_jaxpr/sci,sdj->ijcd/dot_general | solution.py:116
  511.2 32.8 %bitcast_dynamic-update-slice_fusion.4 = f32[8,16,256,128]{3,2,1,0:T(8,128)} fusion(f32[8,16,256,128]{3,2,1,0:T(8,128)} %get-tuple-element.411, s32[]{:T(128)S(6)} %copy.191, f32[16,256,1024]{1,0,2:T(8,128)S(1)} %bitcast.139, f32[1024,128]{1,0:T(8,128)S(1)} %get-tuple-element.425), kind=kOutput, calls=%fused_computation.17.clone.1 | convolution fusion | flops 6442450944 | bytes 19398660 | tf_op jit(solution)/shard_map/while/body/eval_jaxpr/dot_general | solution.py:18
  545.1 14.4 %convolution_multiply_fusion.3 = f32[32,16,32,256]{3,1,2,0:T(8,128)S(1)} fusion(f32[32,32,256]{2,0,1:T(8,128)S(1)} %get-tuple-element.424, f32[32,32,128]{0,2,1:T(8,128)} %get-tuple-element.423, s32[]{:T(128)S(6)} %select_n.9), kind=kOutput, calls=%fused_computation.16.clone.1 | convolution fusion | flops 1614807040 | bytes 18087940 | tf_op jit(solution)/shard_map/while/body/eval_jaxpr/sci,sdj->ijcd/dot_general | solution.py:116
  559.5 32.8 %bitcast_dynamic-update-slice_fusion.4 = f32[8,16,256,128]{3,2,1,0:T(8,128)} fusion(f32[8,16,256,128]{3,2,1,0:T(8,128)} %get-tuple-element.411, s32[]{:T(128)S(6)} %copy.191, f32[16,256,1024]{1,0,2:T(8,128)S(1)} %bitcast.139, f32[1024,128]{1,0:T(8,128)S(1)} %get-tuple-element.425), kind=kOutput, calls=%fused_computation.17.clone.1 | convolution fusion | flops 6442450944 | bytes 19398660 | tf_op jit(solution)/shard_map/while/body/eval_jaxpr/dot_general | solution.py:18
  593.5 14.4 %convolution_multiply_fusion.3 = f32[32,16,32,256]{3,1,2,0:T(8,128)S(1)} fusion(f32[32,32,256]{2,0,1:T(8,128)S(1)} %get-tuple-element.424, f32[32,32,128]{0,2,1:T(8,128)} %get-tuple-element.423, s32[]{:T(128)S(6)} %select_n.9), kind=kOutput, calls=%fused_computation.16.clone.1 | convolution fusion | flops 1614807040 | bytes 18087940 | tf_op jit(solution)/shard_map/while/body/eval_jaxpr/sci,sdj->ijcd/dot_general | solution.py:116
  607.9 32.8 %bitcast_dynamic-update-slice_fusion.4 = f32[8,16,256,128]{3,2,1,0:T(8,128)} fusion(f32[8,16,256,128]{3,2,1,0:T(8,128)} %get-tuple-element.411, s32[]{:T(128)S(6)} %copy.191, f32[16,256,1024]{1,0,2:T(8,128)S(1)} %bitcast.139, f32[1024,128]{1,0:T(8,128)S(1)} %get-tuple-element.425), kind=kOutput, calls=%fused_computation.17.clone.1 | convolution fusion | flops 6442450944 | bytes 19398660 | tf_op jit(solution)/shard_map/while/body/eval_jaxpr/dot_general | solution.py:18
  641.9 14.4 %convolution_multiply_fusion.3 = f32[32,16,32,256]{3,1,2,0:T(8,128)S(1)} fusion(f32[32,32,256]{2,0,1:T(8,128)S(1)} %get-tuple-element.424, f32[32,32,128]{0,2,1:T(8,128)} %get-tuple-element.423, s32[]{:T(128)S(6)} %select_n.9), kind=kOutput, calls=%fused_computation.16.clone.1 | convolution fusion | flops 1614807040 | bytes 18087940 | tf_op jit(solution)/shard_map/while/body/eval_jaxpr/sci,sdj->ijcd/dot_general | solution.py:116
  656.3 32.8 %bitcast_dynamic-update-slice_fusion.4 = f32[8,16,256,128]{3,2,1,0:T(8,128)} fusion(f32[8,16,256,128]{3,2,1,0:T(8,128)} %get-tuple-element.411, s32[]{:T(128)S(6)} %copy.191, f32[16,256,1024]{1,0,2:T(8,128)S(1)} %bitcast.139, f32[1024,128]{1,0:T(8,128)S(1)} %get-tuple-element.425), kind=kOutput, calls=%fused_computation.17.clone.1 | convolution fusion | flops 6442450944 | bytes 19398660 | tf_op jit(solution)/shard_map/while/body/eval_jaxpr/dot_general | solution.py:18
  690.2 14.4 %convolution_multiply_fusion.3 = f32[32,16,32,256]{3,1,2,0:T(8,128)S(1)} fusion(f32[32,32,256]{2,0,1:T(8,128)S(1)} %get-tuple-element.424, f32[32,32,128]{0,2,1:T(8,128)} %get-tuple-element.423, s32[]{:T(128)S(6)} %select_n.9), kind=kOutput, calls=%fused_computation.16.clone.1 | convolution fusion | flops 1614807040 | bytes 18087940 | tf_op jit(solution)/shard_map/while/body/eval_jaxpr/sci,sdj->ijcd/dot_general | solution.py:116
  704.6 32.8 %bitcast_dynamic-update-slice_fusion.4 = f32[8,16,256,128]{3,2,1,0:T(8,128)} fusion(f32[8,16,256,128]{3,2,1,0:T(8,128)} %get-tuple-element.411, s32[]{:T(128)S(6)} %copy.191, f32[16,256,1024]{1,0,2:T(8,128)S(1)} %bitcast.139, f32[1024,128]{1,0:T(8,128)S(1)} %get-tuple-element.425), kind=kOutput, calls=%fused_computation.17.clone.1 | convolution fusion | flops 6442450944 | bytes 19398660 | tf_op jit(solution)/shard_map/while/body/eval_jaxpr/dot_general | solution.py:18
  744.3 11.4 %bitcast_add_fusion = f32[128,256,128]{2,1,0:T(8,128)S(1)} fusion(f32[128,256,128]{2,1,0:T(8,128)} %param.24, f32[8,16,256,128]{3,2,1,0:T(8,128)} %get-tuple-element.104), kind=kLoop, calls=%fused_computation.28 | loop fusion | flops 4194304 | bytes 50331648 | tf_op jit(solution)/shard_map/add | solution.py:124
  755.7 4.7 add_reduce_fusion
  760.4 9.5 %multiply_reduce_fusion = f32[128,256]{1,0:T(8,128)S(1)} fusion(f32[128,256,128]{2,1,0:T(8,128)S(1)} %bitcast_add_fusion, f32[128,256]{1,0:T(8,128)S(1)} %broadcast_multiply_fusion, f32[128]{0:T(128)S(1)} %copy-done.9), kind=kLoop, calls=%fused_computation.31 | loop fusion | flops 16744448 | bytes 17039872 | tf_op jit(solution)/shard_map/reduce_sum | solution.py:13
  770.0 57.5 %fusion.21 = f32[128,256,512]{2,1,0:T(8,128)} fusion(f32[128,256,128]{2,1,0:T(8,128)S(1)} %bitcast_add_fusion, f32[128,256]{1,0:T(8,128)S(1)} %add_rsqrt_fusion, f32[128,256]{1,0:T(8,128)S(1)} %broadcast_multiply_fusion, f32[128]{0:T(128)S(1)} %copy-done.9, f32[128,512]{1,0:T(8,128)S(1)} %copy-done), kind=kOutput, calls=%fused_computation.29 | convolution fusion | flops 25782386688 | bytes 84410880 | tf_op jit(solution)/shard_map/dot_general | solution.py:18
  827.5 59.1 %add_add_fusion = f32[128,256,128]{2,1,0:T(8,128)} fusion(f32[128,256,128]{2,1,0:T(8,128)S(1)} %bitcast_add_fusion, f32[128,256,512]{2,1,0:T(8,128)} %fusion.21, f32[512]{0:T(512)S(1)} %copy-done.10, f32[128]{0:T(128)S(1)} %copy-done.9, f32[512,128]{1,0:T(8,128)S(1)} %copy-done.5), kind=kOutput, calls=%fused_computation.38 | convolution fusion | flops 25811746816 | bytes 100928000 | tf_op jit(solution)/shard_map/dot_general | solution.py:18
  (141 shorter events, 78.8 us)
Async XLA Ops:
  7.2 762.8 %copy-start = (f32[128,512]{1,0:T(8,128)S(1)}, f32[128,512]{1,0:T(8,128)}, u32[]{:S(2)}) copy-start(f32[128,512]{1,0:T(8,128)} %param.37) | copy-start | bytes 786436
  7.2 19.6 %copy-start.11 = (f32[128,8]{0,1:T(8,128)S(1)}, f32[128,8]{0,1:T(8,128)}, u32[]{:S(2)}) copy-start(f32[128,8]{0,1:T(8,128)} %param.30) | copy-start | bytes 12292
  7.2 149.6 %all-gather.3.cloned.1.call-start = ((), (), s32[]{:S(2)}) async-start(), calls=%async_computation.7 | async-start | bytes 9437184 | tf_op jit(solution)/shard_map/all_gather | solution.py:54
  15.5 11.3 %copy-start.1 = (f32[128,256,128]{2,1,0:T(8,128)S(1)}, f32[128,256,128]{2,1,0:T(8,128)}, u32[]{:S(2)}) copy-start(f32[128,256,128]{2,1,0:T(8,128)} %param.24) | copy-start | bytes 50331652
  26.8 48.1 %copy-start.2 = (f32[4,256,256]{2,1,0:T(8,128)S(1)}, f32[4,256,256]{2,1,0:T(8,128)}, u32[]{:S(2)}) copy-start(f32[4,256,256]{2,1,0:T(8,128)} %param.23) | copy-start | bytes 3145732
  26.8 48.7 %copy-start.6 = (f32[256,256]{1,0:T(8,128)S(1)}, f32[256,256]{1,0:T(8,128)}, u32[]{:S(2)}) copy-start(f32[256,256]{1,0:T(8,128)} %param.28) | copy-start | bytes 786436
  26.8 48.7 %copy-start.13 = (f32[256]{0:T(256)S(1)}, f32[256]{0:T(256)}, u32[]{:S(2)}) copy-start(f32[256]{0:T(256)} %param.29) | copy-start | bytes 3076
  77.8 15.9 %all-to-all-start.4 = ((f32[4,256,256]{1,0,2:T(4,128)}), f32[4,256,256]{1,0,2:T(4,128)S(1)}, u32[]{:S(2)}, u32[]{:S(2)}) async-start(f32[4,256,256]{1,0,2:T(4,128)} %copy.114), calls=%async_computation.4 | async-start | bytes 2097152 | tf_op jit(solution)/shard_map/all_to_all | solution.py:59
  93.8 16.7 %all-to-all-start.2 = ((f32[4,256,256]{1,0,2:T(4,128)}), f32[4,256,256]{1,0,2:T(4,128)S(1)}, u32[]{:S(2)}, u32[]{:S(2)}) async-start(f32[4,256,256]{1,0,2:T(4,128)} %copy.109), calls=%async_computation.2 | async-start | bytes 2097152 | tf_op jit(solution)/shard_map/all_to_all | solution.py:58
  110.5 17.6 %all-to-all-start.1 = ((f32[4,256,256]{1,0,2:T(4,128)}), f32[4,256,256]{1,0,2:T(4,128)}, u32[]{:S(2)}, u32[]{:S(2)}) async-start(f32[4,256,256]{1,0,2:T(4,128)} %copy.106), calls=%async_computation.1 | async-start | bytes 2097152 | tf_op jit(solution)/shard_map/all_to_all | solution.py:57
  128.1 17.1 %all-to-all-start = ((f32[4,256,256]{1,0,2:T(4,128)}), f32[4,256,256]{1,0,2:T(4,128)S(1)}, u32[]{:S(2)}, u32[]{:S(2)}) async-start(f32[4,256,256]{1,0,2:T(4,128)} %copy.103), calls=%async_computation | async-start | bytes 2097152 | tf_op jit(solution)/shard_map/all_to_all | solution.py:56
  156.8 122.6 %copy-start.3 = (f32[4,256,256]{2,1,0:T(8,128)S(1)}, f32[4,256,256]{2,1,0:T(8,128)}, u32[]{:S(2)}) copy-start(f32[4,256,256]{2,1,0:T(8,128)} %param.23) | copy-start | bytes 3145732
  268.0 34.8 %copy-start.12 = (f32[256]{0:T(256)S(1)}, f32[256]{0:T(256)}, u32[]{:S(2)}) copy-start(f32[256]{0:T(256)} %param.32) | copy-start | bytes 3076
  268.0 37.7 %copy-start.7 = (f32[256,32]{0,1:T(8,128)S(1)}, f32[256,32]{0,1:T(8,128)}, u32[]{:S(2)}) copy-start(f32[256,32]{0,1:T(8,128)} %param.34) | copy-start | bytes 98308
  268.0 39.2 %copy-start.8 = (f32[256,32]{0,1:T(8,128)S(1)}, f32[256,32]{0,1:T(8,128)}, u32[]{:S(2)}) copy-start(f32[256,32]{0,1:T(8,128)} %param.33) | copy-start | bytes 98308
  275.5 17.8 %all-to-all-start.5 = ((f32[4,1,65536]{2,1,0:T(1,128)}), f32[4,1,65536]{2,1,0:T(1,128)S(1)}, u32[]{:S(2)}, u32[]{:S(2)}) async-start(f32[4,1,65536]{2,1,0:T(1,128)} %reshape.117), calls=%async_computation.5 | async-start | bytes 2097152 | tf_op jit(solution)/shard_map/all_to_all | solution.py:93
  279.1 69.4 %all-gather.5.cloned.1.call-start = ((), (), s32[]{:S(2)}) async-start(), calls=%async_computation.8 | async-start | bytes 1179648 | tf_op jit(solution)/shard_map/all_gather | solution.py:110
  298.5 51.9 %copy-start.4 = (f32[1024,128]{1,0:T(8,128)S(1)}, f32[1024,128]{1,0:T(8,128)}, u32[]{:S(2)}) copy-start(f32[1024,128]{1,0:T(8,128)} %param.35) | copy-start | bytes 1572868
  323.7 19.1 %all-to-all-start.6 = ((f32[8,1,16384]{2,1,0:T(1,128)}), f32[8,1,16384]{2,1,0:T(1,128)S(1)}, u32[]{:S(2)}, u32[]{:S(2)}) async-start(f32[8,1,16384]{2,1,0:T(1,128)} %reshape.119), calls=%async_computation.6 | async-start | bytes 1048576 | tf_op jit(solution)/shard_map/all_to_all | solution.py:105
  744.3 11.4 %copy-start.9 = (f32[128]{0:T(128)S(1)}, f32[128]{0:T(128)}, u32[]{:S(2)}) copy-start(f32[128]{0:T(128)} %param.36) | copy-start | bytes 1540
  769.9 57.5 %copy-start.5 = (f32[512,128]{1,0:T(8,128)S(1)}, f32[512,128]{1,0:T(8,128)}, u32[]{:S(2)}) copy-start(f32[512,128]{1,0:T(8,128)} %param.39) | copy-start | bytes 786436
  769.9 57.5 %copy-start.10 = (f32[512]{0:T(512)S(1)}, f32[512]{0:T(512)}, u32[]{:S(2)}) copy-start(f32[512]{0:T(512)} %param.38) | copy-start | bytes 6148
Sparse Core Ops, SparseCore 0:
  75.0 81.7 all-gather.2
  307.3 19.8 all-gather.4
where the time goes:
time: 902 us; the launch traced here: 894 us
  matrix products  618 us (69%)
  waiting for transfers between devices  70 us (8%)
  other arithmetic  64.1 us (7%)
  local copies, waits for them, and re-layouts  56.5 us (6%)
  blocking collectives  29.6 us (3%)
  starting transfers between devices  23.1 us (3%)
  loops' own time  17.1 us (2%)
  between operations  14.7 us (2%)
    dot_general x15, matrix products, matrix_multiply(): jnp.dot(first_arr, second_arr, precision=finest_precision, preferred_elem...  391 us
    dot_general x8, matrix products, outer_block(): jnp.einsum('sci,sdj->ijcd', left_part, right_all, precision=finest_precis...  115 us
    dot_general x8, matrix products, per_block(): jnp.einsum('qhd,khd->hqk', query_rows, key_item, precision=finest_precision)  45.8 us
    dot_general x8, matrix products, per_block(): jnp.einsum('hqk,khd->qhd', softmax_probabilities, value_item, precision=f...  36.8 us
    dot_general x1, matrix products, per_device(): jnp.einsum('ijc,ch->hij', layer_normalize(pair_state), pair_bias_weight,...  27.4 us
    reduce_sum x4, other arithmetic, layer_normalize(): variance = jnp.mean(centered * centered, axis=-1, keepdims=True)  21.3 us
    all_to_all x1, blocking collectives, per_device(): lax.all_to_all(bias_tile, 'narrow', split_axis=0, concat_axis=2, tiled=True)  19.1 us
  transfers between devices with their start and end apart: 8, of which 7 were waited for; matrix products, arithmetic and copies ran while one was open for 4% of the time, Pallas kernels for 0%

commit v1 on v0

--- a/solution.py
+++ b/solution.py
@@ -102,7 +102,15 @@
         "srm,mc->scr", outer_product_normed, second_factor_projector, precision=finest_precision
     )
     left_rows = lax.all_gather(left_proj, "narrow", axis=2, tiled=True)
-    left_all = lax.all_to_all(left_rows, "wide", split_axis=2, concat_axis=0, tiled=True)
+    left_all = jnp.concatenate(
+        jax.lax.all_to_all(
+            jnp.stack(jnp.split(left_rows, jax.lax.axis_size("wide"), axis=2), axis=0),
+            axis_name="wide",
+            split_axis=0,
+            concat_axis=0,
+        ),
+        axis=0,
+    )
     seq_count = left_all.shape[0]
     tile_rows = left_all.shape[2]
     tile_cols = right_proj.shape[2]

time: 902 us -> 918 us (1.018)
  loops' own time: 17.1 us -> 37.6 us
    another operation x1, loops' own time: 11.5 us -> 32 us  [per_device(): lax.map(outer_block, jnp.arange(tile_rows // block_rows, dtype=jnp.int32))]
where the time goes in v1:
time: 918 us; the launch traced here: 910 us
  matrix products  618 us (67%)
  waiting for transfers between devices  70 us (8%)
  other arithmetic  60.4 us (7%)
  local copies, waits for them, and re-layouts  56.8 us (6%)
  loops' own time  37.6 us (4%)
  blocking collectives  29.6 us (3%)
  starting transfers between devices  22.7 us (2%)
  between operations  14.7 us (2%)
    dot_general x15, matrix products, matrix_multiply(): jnp.dot(first_arr, second_arr, precision=finest_precision, preferred_elem...  391 us
    dot_general x8, matrix products, outer_block(): jnp.einsum('sci,sdj->ijcd', left_part, right_all, precision=finest_precis...  115 us
    dot_general x8, matrix products, per_block(): jnp.einsum('qhd,khd->hqk', query_rows, key_item, precision=finest_precision)  45.8 us
    dot_general x8, matrix products, per_block(): jnp.einsum('hqk,khd->qhd', softmax_probabilities, value_item, precision=f...  36.8 us
    another operation x1, loops' own time, per_device(): lax.map(outer_block, jnp.arange(tile_rows // block_rows, dtype=jnp.int32))  32 us
    dot_general x1, matrix products, per_device(): jnp.einsum('ijc,ch->hij', layer_normalize(pair_state), pair_bias_weight,...  27.4 us
    reduce_sum x4, other arithmetic, layer_normalize(): variance = jnp.mean(centered * centered, axis=-1, keepdims=True)  21.3 us
    all_to_all x1, blocking collectives, per_device(): lax.all_to_all(bias_tile, 'narrow', split_axis=0, concat_axis=2, tiled=True)  19.1 us
  transfers between devices with their start and end apart: 8, of which 7 were waited for; matrix products, arithmetic and copies ran while one was open for 4% of the time, Pallas kernels for 0%

profile of v1, /device:TPU:0, one launch (start us, length us, event | category | flops | bytes accessed | tf_op | source)
XLA Modules:
  0.0 909.9 jit_solution(7289599455200662099)
XLA Ops:
  7.2 8.2 reduce_sum.83
  15.5 11.2 %multiply_reduce_fusion.1 = f32[128,256]{1,0:T(8,128)S(1)} fusion(f32[128,256,128]{2,1,0:T(8,128)} %param.24, f32[128,256]{1,0:T(8,128)S(1)} %broadcast_multiply_fusion.1), kind=kLoop, calls=%fused_computation.34 | loop fusion | flops 12550144 | bytes 17039360 | tf_op jit(solution)/shard_map/reduce_sum | solution.py:13
  26.8 27.4 %fusion.36 = f32[8,128,256]{2,0,1:T(8,128)S(1)} fusion(f32[128,256,128]{2,1,0:T(8,128)S(1)} %copy-done.1, f32[128,256]{1,0:T(8,128)S(1)} %add_rsqrt_fusion.1, f32[128,256]{1,0:T(8,128)S(1)} %broadcast_multiply_fusion.1, f32[128,8]{0,1:T(8,128)S(1)} %copy-done.12), kind=kOutput, calls=%fused_computation.49 | convolution fusion | flops 411041792 | bytes 18092032 | tf_op jit(solution)/shard_map/ijc,ch->hij/dot_general | solution.py:50
  54.6 19.1 %all_to_all.104 = f32[8,128,256]{2,1,0:T(8,128)S(1)} all-to-all(f32[8,128,256]{2,1,0:T(8,128)S(1)} %copy.81), channel_id=1, replica_groups=mesh['wide'=8,'narrow'=4] {'narrow'}, dimensions={0} | all-to-all | bytes 2097152 | tf_op jit(solution)/shard_map/all_to_all | solution.py:53
  77.9 3.5 all-to-all-start.4
  84.7 9.1 all-to-all-done.4
  93.8 3.5 all-to-all-start.2
  102.9 7.6 all-to-all-done.2
  110.5 4.2 all-to-all-start.1
  114.8 3.0 convolution_multiply_fusion.1
  120.3 7.8 all-to-all-done.1
  128.1 4.0 all-to-all-start
  137.5 7.7 all-to-all-done
  145.6 11.2 %all-gather.3.cloned.1.call-done = f32[2,1024,1024]{2,1,0:T(8,128)} async-done(((f32[2,128,1024]{2,1,0:T(8,128)}), f32[2,1024,1024]{2,1,0:T(8,128)}) %all-gather.3.cloned.1.call-update) | async-done | bytes 8388624 | tf_op jit(solution)/shard_map/all_gather | solution.py:54
  156.8 110.9 %while.31 = (s32[]{:T(128)}, f32[4,1024,64]{1,2,0:T(8,128)}, f32[4,1024,64]{1,2,0:T(8,128)S(1)}, f32[4,1024,64]{1,2,0:T(8,128)}, f32[4,1024,64]{1,2,0:T(8,128)},...) while((s32[]{:T(128)}, f32[4,1024,64]{1,2,0:T(8,128)}, ...), condition=%wide.region_9.10_spmd, body=%wide.region_4.9_spmd.sunk | while | flops 811595776 | bytes 20993444 | solution.py:91
  158.0 25.5 %while.33 = (s32[]{:T(128)}, f32[2,512,64]{1,2,0:T(8,128)S(1)}, s32[2]{0:T(128)S(1)}, f32[1024,2,32]{0,2,1:T(8,128)S(1)}, f32[1024,2,32]{0,2,1:T(8,128)S(1)}, /*...) while((s32[]{:T(128)}, f32[2,512,64]{1,2,0:T(8,128)S(1)}, ...), condition=%wide.region_8.8_spmd, body=%wide.region_5.7_spmd.sunk | while | flops 811595776 | bytes 17847476 | solution.py:88
  159.2 5.7 fusion.107
  166.1 4.6 fusion.109
  172.0 5.7 fusion.107
  178.8 4.6 fusion.109
  185.7 25.5 %while.33 = (s32[]{:T(128)}, f32[2,512,64]{1,2,0:T(8,128)S(1)}, s32[2]{0:T(128)S(1)}, f32[1024,2,32]{0,2,1:T(8,128)S(1)}, f32[1024,2,32]{0,2,1:T(8,128)S(1)}, /*...) while((s32[]{:T(128)}, f32[2,512,64]{1,2,0:T(8,128)S(1)}, ...), condition=%wide.region_8.8_spmd, body=%wide.region_5.7_spmd.sunk | while | flops 811595776 | bytes 17847476 | solution.py:88
  186.9 5.7 fusion.107
  193.8 4.6 fusion.109
  199.7 5.7 fusion.107
  206.5 4.6 fusion.109
  213.4 25.5 %while.33 = (s32[]{:T(128)}, f32[2,512,64]{1,2,0:T(8,128)S(1)}, s32[2]{0:T(128)S(1)}, f32[1024,2,32]{0,2,1:T(8,128)S(1)}, f32[1024,2,32]{0,2,1:T(8,128)S(1)}, /*...) while((s32[]{:T(128)}, f32[2,512,64]{1,2,0:T(8,128)S(1)}, ...), condition=%wide.region_8.8_spmd, body=%wide.region_5.7_spmd.sunk | while | flops 811595776 | bytes 17847476 | solution.py:88
  214.6 5.7 fusion.107
  221.5 4.6 fusion.109
  227.4 5.7 fusion.107
  234.2 4.6 fusion.109
  241.1 25.5 %while.33 = (s32[]{:T(128)}, f32[2,512,64]{1,2,0:T(8,128)S(1)}, s32[2]{0:T(128)S(1)}, f32[1024,2,32]{0,2,1:T(8,128)S(1)}, f32[1024,2,32]{0,2,1:T(8,128)S(1)}, /*...) while((s32[]{:T(128)}, f32[2,512,64]{1,2,0:T(8,128)S(1)}, ...), condition=%wide.region_8.8_spmd, body=%wide.region_5.7_spmd.sunk | while | flops 811595776 | bytes 17847476 | solution.py:88
  242.4 5.7 fusion.107
  249.2 4.6 fusion.109
  255.1 5.7 fusion.107
  261.9 4.6 fusion.109
  271.2 4.5 reshape.121
  275.7 3.7 all-to-all-start.5
  280.9 12.6 %all-to-all-done.5 = f32[4,1,65536]{2,1,0:T(1,128)S(1)} async-done(((f32[4,1,65536]{2,1,0:T(1,128)}), f32[4,1,65536]{2,1,0:T(1,128)S(1)}, u32[]{:S(2)}, u32[]{:S(2)}) %all-to-all-start.5) | async-done | bytes 1048608 | tf_op jit(solution)/shard_map/all_to_all | solution.py:93
  294.1 3.7 reduce
  307.3 10.5 %all_gather.10 = f32[4,32,1024]{2,1,0:T(8,128)S(1)} all-gather(f32[4,32,256]{2,1,0:T(8,128)S(1)} %convolution_bitcast_fusion.1), channel_id=1, replica_groups=mesh['wide'=8,'narrow'=4] {'narrow'}, dimensions={2}, use_global_device_ids=true | all-gather | bytes 655360 | tf_op jit(solution)/shard_map/all_gather | solution.py:104
  322.8 3.5 all-to-all-start.6
  327.6 13.9 %all-to-all-done.6 = f32[8,4,32,128]{3,2,1,0:T(8,128)S(1)} async-done(((f32[8,4,32,128]{3,2,1,0:T(8,128)}), f32[8,4,32,128]{3,2,1,0:T(8,128)S(1)}, u32[]{:S(2)}, u32[]{:S(2)}) %all-to-all-start.6) | async-done | bytes 524320 | tf_op jit(solution)/shard_map/all_to_all | solution.py:106
  345.4 415.1 %while.32 = (s32[]{:T(128)}, f32[8,16,256,128]{3,2,1,0:T(8,128)}, s32[8]{0:T(128)S(1)}, f32[32,32,128]{0,2,1:T(8,128)}, f32[32,32,256]{2,0,1:T(8,128)S(1)}, /*in...) while((s32[]{:T(128)}, f32[8,16,256,128]{3,2,1,0:T(8,128)}, ...), condition=%wide.region_13.14_spmd, body=%wide.region_12.13_spmd.sunk | while | flops 8057257984 | bytes 37486768 | solution.py:130
  366.4 14.4 %convolution_multiply_fusion.3 = f32[32,16,32,256]{3,1,2,0:T(8,128)S(1)} fusion(f32[32,32,256]{2,0,1:T(8,128)S(1)} %get-tuple-element.416, f32[32,32,128]{0,2,1:T(8,128)} %get-tuple-element.415, s32[]{:T(128)S(6)} %select_n.9), kind=kOutput, calls=%fused_computation.16.clone.1 | convolution fusion | flops 1614807040 | bytes 18087940 | tf_op jit(solution)/shard_map/while/body/eval_jaxpr/sci,sdj->ijcd/dot_general | solution.py:124
  380.8 32.8 %bitcast_dynamic-update-slice_fusion.4 = f32[8,16,256,128]{3,2,1,0:T(8,128)} fusion(f32[8,16,256,128]{3,2,1,0:T(8,128)} %get-tuple-element.403, s32[]{:T(128)S(6)} %copy.162, f32[16,256,1024]{1,0,2:T(8,128)S(1)} %bitcast.165, f32[1024,128]{1,0:T(8,128)S(1)} %get-tuple-element.417), kind=kOutput, calls=%fused_computation.17.clone.1 | convolution fusion | flops 6442450944 | bytes 19398660 | tf_op jit(solution)/shard_map/while/body/eval_jaxpr/dot_general | solution.py:18
  415.0 14.4 %convolution_multiply_fusion.3 = f32[32,16,32,256]{3,1,2,0:T(8,128)S(1)} fusion(f32[32,32,256]{2,0,1:T(8,128)S(1)} %get-tuple-element.416, f32[32,32,128]{0,2,1:T(8,128)} %get-tuple-element.415, s32[]{:T(128)S(6)} %select_n.9), kind=kOutput, calls=%fused_computation.16.clone.1 | convolution fusion | flops 1614807040 | bytes 18087940 | tf_op jit(solution)/shard_map/while/body/eval_jaxpr/sci,sdj->ijcd/dot_general | solution.py:124
  429.4 32.8 %bitcast_dynamic-update-slice_fusion.4 = f32[8,16,256,128]{3,2,1,0:T(8,128)} fusion(f32[8,16,256,128]{3,2,1,0:T(8,128)} %get-tuple-element.403, s32[]{:T(128)S(6)} %copy.162, f32[16,256,1024]{1,0,2:T(8,128)S(1)} %bitcast.165, f32[1024,128]{1,0:T(8,128)S(1)} %get-tuple-element.417), kind=kOutput, calls=%fused_computation.17.clone.1 | convolution fusion | flops 6442450944 | bytes 19398660 | tf_op jit(solution)/shard_map/while/body/eval_jaxpr/dot_general | solution.py:18
  463.6 14.4 %convolution_multiply_fusion.3 = f32[32,16,32,256]{3,1,2,0:T(8,128)S(1)} fusion(f32[32,32,256]{2,0,1:T(8,128)S(1)} %get-tuple-element.416, f32[32,32,128]{0,2,1:T(8,128)} %get-tuple-element.415, s32[]{:T(128)S(6)} %select_n.9), kind=kOutput, calls=%fused_computation.16.clone.1 | convolution fusion | flops 1614807040 | bytes 18087940 | tf_op jit(solution)/shard_map/while/body/eval_jaxpr/sci,sdj->ijcd/dot_general | solution.py:124
  478.0 32.8 %bitcast_dynamic-update-slice_fusion.4 = f32[8,16,256,128]{3,2,1,0:T(8,128)} fusion(f32[8,16,256,128]{3,2,1,0:T(8,128)} %get-tuple-element.403, s32[]{:T(128)S(6)} %copy.162, f32[16,256,1024]{1,0,2:T(8,128)S(1)} %bitcast.165, f32[1024,128]{1,0:T(8,128)S(1)} %get-tuple-element.417), kind=kOutput, calls=%fused_computation.17.clone.1 | convolution fusion | flops 6442450944 | bytes 19398660 | tf_op jit(solution)/shard_map/while/body/eval_jaxpr/dot_general | solution.py:18
  512.1 14.4 %convolution_multiply_fusion.3 = f32[32,16,32,256]{3,1,2,0:T(8,128)S(1)} fusion(f32[32,32,256]{2,0,1:T(8,128)S(1)} %get-tuple-element.416, f32[32,32,128]{0,2,1:T(8,128)} %get-tuple-element.415, s32[]{:T(128)S(6)} %select_n.9), kind=kOutput, calls=%fused_computation.16.clone.1 | convolution fusion | flops 1614807040 | bytes 18087940 | tf_op jit(solution)/shard_map/while/body/eval_jaxpr/sci,sdj->ijcd/dot_general | solution.py:124
  526.5 32.8 %bitcast_dynamic-update-slice_fusion.4 = f32[8,16,256,128]{3,2,1,0:T(8,128)} fusion(f32[8,16,256,128]{3,2,1,0:T(8,128)} %get-tuple-element.403, s32[]{:T(128)S(6)} %copy.162, f32[16,256,1024]{1,0,2:T(8,128)S(1)} %bitcast.165, f32[1024,128]{1,0:T(8,128)S(1)} %get-tuple-element.417), kind=kOutput, calls=%fused_computation.17.clone.1 | convolution fusion | flops 6442450944 | bytes 19398660 | tf_op jit(solution)/shard_map/while/body/eval_jaxpr/dot_general | solution.py:18
  560.7 14.4 %convolution_multiply_fusion.3 = f32[32,16,32,256]{3,1,2,0:T(8,128)S(1)} fusion(f32[32,32,256]{2,0,1:T(8,128)S(1)} %get-tuple-element.416, f32[32,32,128]{0,2,1:T(8,128)} %get-tuple-element.415, s32[]{:T(128)S(6)} %select_n.9), kind=kOutput, calls=%fused_computation.16.clone.1 | convolution fusion | flops 1614807040 | bytes 18087940 | tf_op jit(solution)/shard_map/while/body/eval_jaxpr/sci,sdj->ijcd/dot_general | solution.py:124
  575.1 32.8 %bitcast_dynamic-update-slice_fusion.4 = f32[8,16,256,128]{3,2,1,0:T(8,128)} fusion(f32[8,16,256,128]{3,2,1,0:T(8,128)} %get-tuple-element.403, s32[]{:T(128)S(6)} %copy.162, f32[16,256,1024]{1,0,2:T(8,128)S(1)} %bitcast.165, f32[1024,128]{1,0:T(8,128)S(1)} %get-tuple-element.417), kind=kOutput, calls=%fused_computation.17.clone.1 | convolution fusion | flops 6442450944 | bytes 19398660 | tf_op jit(solution)/shard_map/while/body/eval_jaxpr/dot_general | solution.py:18
  609.3 14.4 %convolution_multiply_fusion.3 = f32[32,16,32,256]{3,1,2,0:T(8,128)S(1)} fusion(f32[32,32,256]{2,0,1:T(8,128)S(1)} %get-tuple-element.416, f32[32,32,128]{0,2,1:T(8,128)} %get-tuple-element.415, s32[]{:T(128)S(6)} %select_n.9), kind=kOutput, calls=%fused_computation.16.clone.1 | convolution fusion | flops 1614807040 | bytes 18087940 | tf_op jit(solution)/shard_map/while/body/eval_jaxpr/sci,sdj->ijcd/dot_general | solution.py:124
  623.7 32.8 %bitcast_dynamic-update-slice_fusion.4 = f32[8,16,256,128]{3,2,1,0:T(8,128)} fusion(f32[8,16,256,128]{3,2,1,0:T(8,128)} %get-tuple-element.403, s32[]{:T(128)S(6)} %copy.162, f32[16,256,1024]{1,0,2:T(8,128)S(1)} %bitcast.165, f32[1024,128]{1,0:T(8,128)S(1)} %get-tuple-element.417), kind=kOutput, calls=%fused_computation.17.clone.1 | convolution fusion | flops 6442450944 | bytes 19398660 | tf_op jit(solution)/shard_map/while/body/eval_jaxpr/dot_general | solution.py:18
  657.9 14.4 %convolution_multiply_fusion.3 = f32[32,16,32,256]{3,1,2,0:T(8,128)S(1)} fusion(f32[32,32,256]{2,0,1:T(8,128)S(1)} %get-tuple-element.416, f32[32,32,128]{0,2,1:T(8,128)} %get-tuple-element.415, s32[]{:T(128)S(6)} %select_n.9), kind=kOutput, calls=%fused_computation.16.clone.1 | convolution fusion | flops 1614807040 | bytes 18087940 | tf_op jit(solution)/shard_map/while/body/eval_jaxpr/sci,sdj->ijcd/dot_general | solution.py:124
  672.3 32.8 %bitcast_dynamic-update-slice_fusion.4 = f32[8,16,256,128]{3,2,1,0:T(8,128)} fusion(f32[8,16,256,128]{3,2,1,0:T(8,128)} %get-tuple-element.403, s32[]{:T(128)S(6)} %copy.162, f32[16,256,1024]{1,0,2:T(8,128)S(1)} %bitcast.165, f32[1024,128]{1,0:T(8,128)S(1)} %get-tuple-element.417), kind=kOutput, calls=%fused_computation.17.clone.1 | convolution fusion | flops 6442450944 | bytes 19398660 | tf_op jit(solution)/shard_map/while/body/eval_jaxpr/dot_general | solution.py:18
  706.5 14.4 %convolution_multiply_fusion.3 = f32[32,16,32,256]{3,1,2,0:T(8,128)S(1)} fusion(f32[32,32,256]{2,0,1:T(8,128)S(1)} %get-tuple-element.416, f32[32,32,128]{0,2,1:T(8,128)} %get-tuple-element.415, s32[]{:T(128)S(6)} %select_n.9), kind=kOutput, calls=%fused_computation.16.clone.1 | convolution fusion | flops 1614807040 | bytes 18087940 | tf_op jit(solution)/shard_map/while/body/eval_jaxpr/sci,sdj->ijcd/dot_general | solution.py:124
  720.9 32.8 %bitcast_dynamic-update-slice_fusion.4 = f32[8,16,256,128]{3,2,1,0:T(8,128)} fusion(f32[8,16,256,128]{3,2,1,0:T(8,128)} %get-tuple-element.403, s32[]{:T(128)S(6)} %copy.162, f32[16,256,1024]{1,0,2:T(8,128)S(1)} %bitcast.165, f32[1024,128]{1,0:T(8,128)S(1)} %get-tuple-element.417), kind=kOutput, calls=%fused_computation.17.clone.1 | convolution fusion | flops 6442450944 | bytes 19398660 | tf_op jit(solution)/shard_map/while/body/eval_jaxpr/dot_general | solution.py:18
  760.6 11.4 %bitcast_add_fusion = f32[128,256,128]{2,1,0:T(8,128)S(1)} fusion(f32[128,256,128]{2,1,0:T(8,128)} %param.24, f32[8,16,256,128]{3,2,1,0:T(8,128)} %get-tuple-element.104), kind=kLoop, calls=%fused_computation.28 | loop fusion | flops 4194304 | bytes 50331648 | tf_op jit(solution)/shard_map/add | solution.py:132
  771.9 4.7 add_reduce_fusion
  776.6 9.5 %multiply_reduce_fusion = f32[128,256]{1,0:T(8,128)S(1)} fusion(f32[128,256,128]{2,1,0:T(8,128)S(1)} %bitcast_add_fusion, f32[128,256]{1,0:T(8,128)S(1)} %broadcast_multiply_fusion, f32[128]{0:T(128)S(1)} %copy-done.10), kind=kLoop, calls=%fused_computation.31 | loop fusion | flops 16744448 | bytes 17039872 | tf_op jit(solution)/shard_map/reduce_sum | solution.py:13
  786.2 57.5 %fusion.21 = f32[128,256,512]{2,1,0:T(8,128)} fusion(f32[128,256,128]{2,1,0:T(8,128)S(1)} %bitcast_add_fusion, f32[128,256]{1,0:T(8,128)S(1)} %add_rsqrt_fusion, f32[128,256]{1,0:T(8,128)S(1)} %broadcast_multiply_fusion, f32[128]{0:T(128)S(1)} %copy-done.10, f32[128,512]{1,0:T(8,128)S(1)} %copy-done), kind=kOutput, calls=%fused_computation.29 | convolution fusion | flops 25782386688 | bytes 84410880 | tf_op jit(solution)/shard_map/dot_general | solution.py:18
  843.8 59.1 %add_add_fusion = f32[128,256,128]{2,1,0:T(8,128)} fusion(f32[128,256,128]{2,1,0:T(8,128)S(1)} %bitcast_add_fusion, f32[128,256,512]{2,1,0:T(8,128)} %fusion.21, f32[512]{0:T(512)S(1)} %copy-done.11, f32[128]{0:T(128)S(1)} %copy-done.10, f32[512,128]{1,0:T(8,128)S(1)} %copy-done.5), kind=kOutput, calls=%fused_computation.38 | convolution fusion | flops 25811746816 | bytes 100928000 | tf_op jit(solution)/shard_map/dot_general | solution.py:18
  (146 shorter events, 74.9 us)
Async XLA Ops:
  7.2 779.0 %copy-start = (f32[128,512]{1,0:T(8,128)S(1)}, f32[128,512]{1,0:T(8,128)}, u32[]{:S(2)}) copy-start(f32[128,512]{1,0:T(8,128)} %param.37) | copy-start | bytes 786436
  7.2 19.6 %copy-start.12 = (f32[128,8]{0,1:T(8,128)S(1)}, f32[128,8]{0,1:T(8,128)}, u32[]{:S(2)}) copy-start(f32[128,8]{0,1:T(8,128)} %param.30) | copy-start | bytes 12292
  7.2 149.6 %all-gather.3.cloned.1.call-start = ((), (), s32[]{:S(2)}) async-start(), calls=%async_computation.7 | async-start | bytes 9437184 | tf_op jit(solution)/shard_map/all_gather | solution.py:54
  15.5 11.3 %copy-start.1 = (f32[128,256,128]{2,1,0:T(8,128)S(1)}, f32[128,256,128]{2,1,0:T(8,128)}, u32[]{:S(2)}) copy-start(f32[128,256,128]{2,1,0:T(8,128)} %param.24) | copy-start | bytes 50331652
  26.8 48.1 %copy-start.2 = (f32[4,256,256]{2,1,0:T(8,128)S(1)}, f32[4,256,256]{2,1,0:T(8,128)}, u32[]{:S(2)}) copy-start(f32[4,256,256]{2,1,0:T(8,128)} %param.23) | copy-start | bytes 3145732
  26.8 48.7 %copy-start.6 = (f32[256,256]{1,0:T(8,128)S(1)}, f32[256,256]{1,0:T(8,128)}, u32[]{:S(2)}) copy-start(f32[256,256]{1,0:T(8,128)} %param.28) | copy-start | bytes 786436
  26.8 48.7 %copy-start.14 = (f32[256]{0:T(256)S(1)}, f32[256]{0:T(256)}, u32[]{:S(2)}) copy-start(f32[256]{0:T(256)} %param.29) | copy-start | bytes 3076
  77.9 15.9 %all-to-all-start.4 = ((f32[4,256,256]{1,0,2:T(4,128)}), f32[4,256,256]{1,0,2:T(4,128)S(1)}, u32[]{:S(2)}, u32[]{:S(2)}) async-start(f32[4,256,256]{1,0,2:T(4,128)} %copy.83), calls=%async_computation.4 | async-start | bytes 2097152 | tf_op jit(solution)/shard_map/all_to_all | solution.py:59
  93.8 16.7 %all-to-all-start.2 = ((f32[4,256,256]{1,0,2:T(4,128)}), f32[4,256,256]{1,0,2:T(4,128)S(1)}, u32[]{:S(2)}, u32[]{:S(2)}) async-start(f32[4,256,256]{1,0,2:T(4,128)} %copy.78), calls=%async_computation.2 | async-start | bytes 2097152 | tf_op jit(solution)/shard_map/all_to_all | solution.py:58
  110.5 17.6 %all-to-all-start.1 = ((f32[4,256,256]{1,0,2:T(4,128)}), f32[4,256,256]{1,0,2:T(4,128)}, u32[]{:S(2)}, u32[]{:S(2)}) async-start(f32[4,256,256]{1,0,2:T(4,128)} %copy.75), calls=%async_computation.1 | async-start | bytes 2097152 | tf_op jit(solution)/shard_map/all_to_all | solution.py:57
  128.1 17.1 %all-to-all-start = ((f32[4,256,256]{1,0,2:T(4,128)}), f32[4,256,256]{1,0,2:T(4,128)S(1)}, u32[]{:S(2)}, u32[]{:S(2)}) async-start(f32[4,256,256]{1,0,2:T(4,128)} %copy.72), calls=%async_computation | async-start | bytes 2097152 | tf_op jit(solution)/shard_map/all_to_all | solution.py:56
  156.8 122.8 %copy-start.3 = (f32[4,256,256]{2,1,0:T(8,128)S(1)}, f32[4,256,256]{2,1,0:T(8,128)}, u32[]{:S(2)}) copy-start(f32[4,256,256]{2,1,0:T(8,128)} %param.23) | copy-start | bytes 3145732
  267.7 34.7 %copy-start.7 = (f32[256,256]{1,0:T(8,128)S(1)}, f32[256,256]{1,0:T(8,128)}, u32[]{:S(2)}) copy-start(f32[256,256]{1,0:T(8,128)} %param.31) | copy-start | bytes 786436
  267.7 34.7 %copy-start.13 = (f32[256]{0:T(256)S(1)}, f32[256]{0:T(256)}, u32[]{:S(2)}) copy-start(f32[256]{0:T(256)} %param.32) | copy-start | bytes 3076
  267.7 37.3 %copy-start.8 = (f32[256,32]{0,1:T(8,128)S(1)}, f32[256,32]{0,1:T(8,128)}, u32[]{:S(2)}) copy-start(f32[256,32]{0,1:T(8,128)} %param.34) | copy-start | bytes 98308
  267.7 38.7 %copy-start.9 = (f32[256,32]{0,1:T(8,128)S(1)}, f32[256,32]{0,1:T(8,128)}, u32[]{:S(2)}) copy-start(f32[256,32]{0,1:T(8,128)} %param.33) | copy-start | bytes 98308
  271.2 74.3 %copy-start.4 = (f32[1024,128]{1,0:T(8,128)S(1)}, f32[1024,128]{1,0:T(8,128)}, u32[]{:S(2)}) copy-start(f32[1024,128]{1,0:T(8,128)} %param.35) | copy-start | bytes 1572868
  275.7 17.8 %all-to-all-start.5 = ((f32[4,1,65536]{2,1,0:T(1,128)}), f32[4,1,65536]{2,1,0:T(1,128)S(1)}, u32[]{:S(2)}, u32[]{:S(2)}) async-start(f32[4,1,65536]{2,1,0:T(1,128)} %reshape.121), calls=%async_computation.5 | async-start | bytes 2097152 | tf_op jit(solution)/shard_map/all_to_all | solution.py:93
  279.4 64.2 %all-gather.5.cloned.1.call-start = ((), (), s32[]{:S(2)}) async-start(), calls=%async_computation.8 | async-start | bytes 1179648 | tf_op jit(solution)/shard_map/all_gather | solution.py:118
  322.8 18.8 %all-to-all-start.6 = ((f32[8,4,32,128]{3,2,1,0:T(8,128)}), f32[8,4,32,128]{3,2,1,0:T(8,128)S(1)}, u32[]{:S(2)}, u32[]{:S(2)}) async-start(f32[8,4,32,128]{3,2,1,0:T(8,128)} %fusion.67), calls=%async_computation.6 | async-start | bytes 1048576 | tf_op jit(solution)/shard_map/all_to_all | solution.py:106
  760.5 11.4 %copy-start.10 = (f32[128]{0:T(128)S(1)}, f32[128]{0:T(128)}, u32[]{:S(2)}) copy-start(f32[128]{0:T(128)} %param.36) | copy-start | bytes 1540
  786.2 57.5 %copy-start.5 = (f32[512,128]{1,0:T(8,128)S(1)}, f32[512,128]{1,0:T(8,128)}, u32[]{:S(2)}) copy-start(f32[512,128]{1,0:T(8,128)} %param.39) | copy-start | bytes 786436
  786.2 57.5 %copy-start.11 = (f32[512]{0:T(512)S(1)}, f32[512]{0:T(512)}, u32[]{:S(2)}) copy-start(f32[512]{0:T(512)} %param.38) | copy-start | bytes 6148
Sparse Core Ops, SparseCore 0:
  75.0 81.7 all-gather.2
  306.6 19.8 all-gather.4
